TPU v7x, 32 devices: a whole 2x2x4 slice. The times are simulated.
32 devices in a mesh: samp: 4 (over x, core), pos: 8 (over z, y).
Axes of the slice: x: 2, y: 2, z: 4, core: 2. Of those that a mesh axis runs over, the one named last changes fastest.
Arguments:
- dosages: bfloat16 [16384, 8192], P('samp', 'pos'), may hold values from -64 to 64
- phenotypes: bfloat16 [16384, 3072], P('samp', 'pos'), may hold values from -64 to 64
- window_low: int32 [3072], P('pos'), may hold values from 0 to 8191, as said below
- window_high: int32 [3072], P('pos'), may hold values from 0 to 8191, as said below
Outputs:
- statistics: float32 [8, 2048, 384], P('pos', 'samp')
Inputs may be any that keep to these rules, and one draw needn't show every extreme that they name: For peak p in block b = p // 384: b * 1024 - 512 <= window_low[p] <= window_high[p] <= b * 1024 + 1535. In every block but the first, one window starts exactly 512 variants before the block; in every block but the last, one ends exactly 512 variants after it. Same bounds as window_low; window_high[p] >= window_low[p].
All inputs are finite; a program needn't handle non-finite values.
Results may differ from a plain program's by a relative error of at most 0.0003.
Values may be sent and summed in bfloat16 or wider, within the bound.
No kernel may reach another device: no remote copies, remote signals or barrier semaphores. Data moves between devices by JAX's collectives and lax.ppermute only.
A program may use at most 64 MiB of HBM per device.

v0:
```python
import math
import jax
import jax.numpy as jnp
from jax import lax
from jax.sharding import PartitionSpec as P

HALO = 512
EPS = 1e-06


def padded(cells, sides, width):
    for axis, dim in sides:
        count = lax.axis_size(axis)
        ends = count - 1
        head = lax.slice_in_dim(cells, 0, width, axis=dim)
        tail = lax.slice_in_dim(cells, cells.shape[dim] - width, cells.shape[dim], axis=dim)
        cells = jnp.concatenate(
            [
                lax.ppermute(tail, axis, [(i, (i + 1) % count) for i in range(ends)]),
                cells,
                lax.ppermute(head, axis, [((i + 1) % count, i) for i in range(ends)]),
            ],
            axis=dim,
        )
    return cells


def from_behind(array, axis, by):
    devices = lax.axis_size(axis)
    pairs = [(i, i + by) for i in range(devices) if 0 <= i + by < devices]
    return lax.ppermute(array, axis, pairs)


def sum_squares(values):
    return jnp.sum(jnp.square(values.astype(jnp.float32)), axis=0)


def cross_rows(variant_panel, phenotypes):
    return lax.dot_general(
        variant_panel, phenotypes, (((0,), (0,)), ((), ())), preferred_element_type=jnp.float32
    )


def shards(dosages, phenotypes, window_low, window_high):
    sample_rows, block_width = dosages.shape
    peak_width = phenotypes.shape[1]
    span_width = block_width + 2 * HALO
    samp_count = lax.axis_size("samp")
    samp_index = lax.axis_index("samp")
    pos_index = lax.axis_index("pos")
    share_rows = span_width // samp_count
    own_first = samp_index * share_rows
    peak_squares = sum_squares(phenotypes)
    near_peaks = padded(phenotypes, (("pos", 1),), peak_width)
    own_tile = cross_rows(dosages, phenotypes)
    lower_edge = cross_rows(dosages[:, :HALO], near_peaks[:, :peak_width])
    upper_edge = cross_rows(dosages[:, block_width - HALO :], near_peaks[:, 2 * peak_width :])
    from_below = from_behind(upper_edge, "pos", 1)
    from_above = from_behind(lower_edge, "pos", -1)
    assembled = jnp.concatenate([from_below, own_tile, from_above], axis=0)
    owned_squares, peak_total = lax.psum((sum_squares(dosages), peak_squares), "samp")
    variant_total = padded(owned_squares, (("pos", 0),), HALO)
    cross_total = lax.psum(assembled, "samp")
    cross_share = lax.dynamic_slice_in_dim(cross_total, own_first, share_rows, 0)
    variant_share = lax.dynamic_slice_in_dim(variant_total, own_first, share_rows, 0)
    variant_index = (
        pos_index * block_width
        - HALO
        + own_first
        + jnp.arange(share_rows, dtype=jnp.int32)[:, None]
    )
    inside = (variant_index >= window_low[None, :]) & (variant_index <= window_high[None, :])
    factor = math.sqrt(float(sample_rows * samp_count - 2))
    scale_terms = (variant_share[:, None] + EPS) * (peak_total[None, :] + EPS)
    statistic = factor * cross_share / jnp.sqrt(scale_terms)
    return jnp.where(inside, statistic, jnp.zeros_like(statistic))[None]


def solution(mesh):
    placed = (P("samp", "pos"), P("samp", "pos"), P("pos"), P("pos"))
    return jax.shard_map(
        shards, mesh=mesh, in_specs=placed, out_specs=P("pos", "samp", None), check_vma=False
    )
```

profile of v0, /device:TPU:0, one launch (start us, length us, event | category | flops | bytes accessed | tf_op | source)
XLA Modules:
  0.0 270.4 jit_solution(13024341628665601439)
XLA Ops:
  6.5 0.0 all-reduce.3.cloned.1.call-start
  6.5 0.0 copy-start
  6.5 5.4 %collective-permute-start.2 = (bf16[4096,384]{1,0:T(8,128)(2,1)}, bf16[4096,384]{1,0:T(8,128)(2,1)S(1)}, u32[]{:S(2)}, u32[]{:S(2)}) collective-permute-start(bf16[4096,384]{1,0:T(8,128)(2,1)} %param.5), channel_id=1, source_target_pairs={{0,1},{1,2},{2,3},{3,4},{4,5},{5,6},{6,7},{8,9},{9,10},{10,11},{11... | collective-permute-start | bytes 9437192 | tf_op jit(solution)/shard_map/ppermute | solution.py:19
  11.9 1.3 collective-permute-start
  13.2 133.6 %collective-permute-done.2 = bf16[4096,384]{1,0:T(8,128)(2,1)S(1)} collective-permute-done((bf16[4096,384]{1,0:T(8,128)(2,1)}, bf16[4096,384]{1,0:T(8,128)(2,1)S(1)}, u32[]{:S(2)}, u32[]{:S(2)}) %collective-permute-start.2) | collective-permute-done | bytes 3145760 | tf_op jit(solution)/shard_map/ppermute | solution.py:19
  146.8 4.5 %fusion = f32[512,384]{1,0:T(8,128)S(1)} fusion(bf16[4096,384]{1,0:T(8,128)(2,1)S(1)} %collective-permute-done.2, bf16[4096,1024]{1,0:T(8,128)(2,1)} %param.4), kind=kOutput, calls=%fused_computation.2 | convolution fusion | flops 1610612736 | bytes 8126464 | tf_op jit(solution)/shard_map/dot_general | solution.py:39
  151.3 0.0 copy-start.1
  151.3 1.6 collective-permute-start.3
  152.9 0.0 collective-permute-done
  152.9 0.0 copy-done
  152.9 2.4 fusion.2
  155.3 5.0 %collective-permute-start.1 = (f32[512,384]{1,0:T(8,128)S(1)}, f32[512,384]{1,0:T(8,128)S(1)}, u32[]{:S(2)}, u32[]{:S(2)}) collective-permute-start(f32[512,384]{1,0:T(8,128)S(1)} %fusion.2), channel_id=1, source_target_pairs={{0,1},{1,2},{2,3},{3,4},{4,5},{5,6},{6,7},{8,9},{9,10},{10,11},{11... | collective-permute-start | bytes 2359304 | tf_op jit(solution)/shard_map/ppermute | solution.py:31
  160.3 0.0 copy-done.1
  160.3 4.5 %fusion.8 = f32[1024,384]{1,0:T(8,128)S(1)} fusion(bf16[4096,1024]{1,0:T(8,128)(2,1)S(1)} %copy-done, bf16[4096,384]{1,0:T(8,128)(2,1)S(1)} %copy-done.1), kind=kOutput, calls=%fused_computation.17 | convolution fusion | flops 3221225472 | bytes 13107200 | tf_op jit(solution)/shard_map/dot_general | solution.py:39
  164.8 7.7 %collective-permute-done.3 = f32[512,384]{1,0:T(8,128)S(1)} collective-permute-done((f32[512,384]{1,0:T(8,128)S(1)}, f32[512,384]{1,0:T(8,128)S(1)}, u32[]{:S(2)}, u32[]{:S(2)}) %collective-permute-start.3) | collective-permute-done | bytes 786464 | tf_op jit(solution)/shard_map/ppermute | solution.py:31
  172.6 17.0 %collective-permute-done.1 = f32[512,384]{1,0:T(8,128)S(1)} collective-permute-done((f32[512,384]{1,0:T(8,128)S(1)}, f32[512,384]{1,0:T(8,128)S(1)}, u32[]{:S(2)}, u32[]{:S(2)}) %collective-permute-start.1) | collective-permute-done | bytes 786464 | tf_op jit(solution)/shard_map/ppermute | solution.py:31
  189.6 1.9 pad_maximum_fusion
  191.4 0.0 all-reduce.3.cloned.1.call-update
  191.4 0.8 multiply_reduce_fusion.1
  192.2 0.0 copy-start.2
  192.2 0.0 copy-start.3
  192.2 5.1 %multiply_reduce_fusion = f32[1024]{0:T(1024)S(1)} fusion(bf16[4096,1024]{1,0:T(8,128)(2,1)} %param.4), kind=kLoop, calls=%fused_computation | loop fusion | flops 12581888 | bytes 8392704 | tf_op jit(solution)/shard_map/reduce_sum | solution.py:35
  197.3 7.8 %all-reduce = (f32[384]{0:T(512)S(1)}, f32[1024]{0:T(1024)S(1)}) all-reduce(f32[384]{0:T(512)S(1)} %multiply_reduce_fusion.1, f32[1024]{0:T(1024)S(1)} %multiply_reduce_fusion), channel_id=1, replica_groups=mesh['samp'=4,'pos'=8] {'samp'}, use_global_device_ids=true, to_apply=%region_4.0 | all-reduce | flops 1408 | bytes 11264 | tf_op jit(solution)/shard_map/psum | solution.py:61
  205.1 4.4 %collective-permute-start.4 = (f32[512]{0:T(512)S(1)}, f32[512]{0:T(512)S(1)}, u32[]{:S(2)}, u32[]{:S(2)}) collective-permute-start(f32[512]{0:T(512)S(1)} %get-tuple-element.8), channel_id=1, source_target_pairs={{0,1},{1,2},{2,3},{3,4},{4,5},{5,6},{6,7},{8,9},{9,10},{10,11},{11... | collective-permute-start | bytes 6152 | tf_op jit(solution)/shard_map/ppermute | solution.py:19
  209.5 1.3 collective-permute-start.5
  210.9 0.0 collective-permute-done.4
  210.9 4.1 %collective-permute-done.5 = f32[512]{0:T(512)S(1)} collective-permute-done((f32[512]{0:T(512)S(1)}, f32[512]{0:T(512)S(1)}, u32[]{:S(2)}, u32[]{:S(2)}) %collective-permute-start.5) | collective-permute-done | bytes 2080 | tf_op jit(solution)/shard_map/ppermute | solution.py:21
  215.0 0.1 fusion.6
  215.1 46.1 %all-reduce.3.cloned.1.call-done = f32[2048,384]{1,0:T(8,128)} async-done(((f32[2048,384]{1,0:T(8,128)}), f32[2048,384]{1,0:T(8,128)}) %all-reduce.3.cloned.1.call-update) | async-done | bytes 3145744 | tf_op jit(solution)/shard_map/psum | solution.py:63
  261.2 0.0 copy-done.2
  261.2 0.0 copy-done.3
  261.2 2.3 select_bitcast_fusion
  (3 shorter events, 0.0 us)
Async XLA Ops:
  6.5 254.7 %all-reduce.3.cloned.1.call-start = ((), (), s32[]{:S(2)}) async-start(), calls=%async_computation | async-start | bytes 6291456 | tf_op jit(solution)/shard_map/psum | solution.py:63
  6.5 146.4 %copy-start = (bf16[4096,1024]{1,0:T(8,128)(2,1)S(1)}, bf16[4096,1024]{1,0:T(8,128)(2,1)}, u32[]{:S(2)}) copy-start(bf16[4096,1024]{1,0:T(8,128)(2,1)} %param.4) | copy-start | bytes 25165828
  6.5 140.2 %collective-permute-start.2 = (bf16[4096,384]{1,0:T(8,128)(2,1)}, bf16[4096,384]{1,0:T(8,128)(2,1)S(1)}, u32[]{:S(2)}, u32[]{:S(2)}) collective-permute-start(bf16[4096,384]{1,0:T(8,128)(2,1)} %param.5), channel_id=1, source_target_pairs={{0,1},{1,2},{2,3},{3,4},{4,5},{5,6},{6,7},{8,9},{9,10},{10,11},{11... | collective-permute-start | bytes 9437192 | tf_op jit(solution)/shard_map/ppermute | solution.py:19
  11.9 141.0 %collective-permute-start = (bf16[4096,384]{1,0:T(8,128)(2,1)}, bf16[4096,384]{1,0:T(8,128)(2,1)S(1)}, u32[]{:S(2)}, u32[]{:S(2)}) collective-permute-start(bf16[4096,384]{1,0:T(8,128)(2,1)} %param.5), channel_id=1, source_target_pairs={{1,0},{2,1},{3,2},{4,3},{5,4},{6,5},{7,6},{9,8},{10,9},{11,10},{12... | collective-permute-start | bytes 9437192 | tf_op jit(solution)/shard_map/ppermute | solution.py:21
  151.3 9.0 %copy-start.1 = (bf16[4096,384]{1,0:T(8,128)(2,1)S(1)}, bf16[4096,384]{1,0:T(8,128)(2,1)}, u32[]{:S(2)}) copy-start(bf16[4096,384]{1,0:T(8,128)(2,1)} %param.5) | copy-start | bytes 9437188
  151.3 21.2 %collective-permute-start.3 = (f32[512,384]{1,0:T(8,128)S(1)}, f32[512,384]{1,0:T(8,128)S(1)}, u32[]{:S(2)}, u32[]{:S(2)}) collective-permute-start(f32[512,384]{1,0:T(8,128)S(1)} %fusion), channel_id=1, source_target_pairs={{1,0},{2,1},{3,2},{4,3},{5,4},{6,5},{7,6},{9,8},{10,9},{11,10},{12... | collective-permute-start | bytes 2359304 | tf_op jit(solution)/shard_map/ppermute | solution.py:31
  155.3 34.2 %collective-permute-start.1 = (f32[512,384]{1,0:T(8,128)S(1)}, f32[512,384]{1,0:T(8,128)S(1)}, u32[]{:S(2)}, u32[]{:S(2)}) collective-permute-start(f32[512,384]{1,0:T(8,128)S(1)} %fusion.2), channel_id=1, source_target_pairs={{0,1},{1,2},{2,3},{3,4},{4,5},{5,6},{6,7},{8,9},{9,10},{10,11},{11... | collective-permute-start | bytes 2359304 | tf_op jit(solution)/shard_map/ppermute | solution.py:31
  192.2 69.0 %copy-start.2 = (s32[384]{0:T(512)S(1)}, s32[384]{0:T(512)}, u32[]{:S(2)}) copy-start(s32[384]{0:T(512)} %param.7) | copy-start | bytes 4612
  192.2 69.0 %copy-start.3 = (s32[384]{0:T(512)S(1)}, s32[384]{0:T(512)}, u32[]{:S(2)}) copy-start(s32[384]{0:T(512)} %param.6) | copy-start | bytes 4612
  205.1 5.7 %collective-permute-start.4 = (f32[512]{0:T(512)S(1)}, f32[512]{0:T(512)S(1)}, u32[]{:S(2)}, u32[]{:S(2)}) collective-permute-start(f32[512]{0:T(512)S(1)} %get-tuple-element.8), channel_id=1, source_target_pairs={{0,1},{1,2},{2,3},{3,4},{4,5},{5,6},{6,7},{8,9},{9,10},{10,11},{11... | collective-permute-start | bytes 6152 | tf_op jit(solution)/shard_map/ppermute | solution.py:19
  209.5 5.5 %collective-permute-start.5 = (f32[512]{0:T(512)S(1)}, f32[512]{0:T(512)S(1)}, u32[]{:S(2)}, u32[]{:S(2)}) collective-permute-start(f32[512]{0:T(512)S(1)} %get-tuple-element.7), channel_id=1, source_target_pairs={{1,0},{2,1},{3,2},{4,3},{5,4},{6,5},{7,6},{9,8},{10,9},{11,10},{12... | collective-permute-start | bytes 6152 | tf_op jit(solution)/shard_map/ppermute | solution.py:21
Sparse Core Ops, SparseCore 0:
  191.6 69.6 all-reduce.2
where the time goes:
time: 271 us; the launch traced here: 270 us
  waiting for transfers between devices  209 us (77%)
  starting transfers between devices  18.8 us (7%)
  between operations  13.5 us (5%)
  matrix products  11.5 us (4%)
  other arithmetic  10.1 us (4%)
  blocking collectives  7.8 us (3%)
    ppermute x2, waiting for transfers between devices, padded(): lax.ppermute(tail, axis, [(i, (i + 1) % count) for i in range(ends)])  134 us
    psum x1, waiting for transfers between devices, shards(): cross_total = lax.psum(assembled, 'samp')  46.1 us
    ppermute x2, waiting for transfers between devices, from_behind(): return lax.ppermute(array, axis, pairs)  24.7 us
    dot_general x3, matrix products, cross_rows(): lax.dot_general(variant_panel, phenotypes, (((0,), (0,)), ((), ())), pref...  11.5 us
    ppermute x2, starting transfers between devices, padded(): lax.ppermute(tail, axis, [(i, (i + 1) % count) for i in range(ends)])  9.74 us
    psum x1, blocking collectives, shards(): lax.psum((sum_squares(dosages), peak_squares), 'samp')  7.8 us
    ppermute x2, starting transfers between devices, from_behind(): return lax.ppermute(array, axis, pairs)  6.51 us
    reduce_sum x2, other arithmetic, sum_squares(): return jnp.sum(jnp.square(values.astype(jnp.float32)), axis=0)  5.86 us
  transfers between devices with their start and end apart: 7, of which 5 were waited for; matrix products, arithmetic and copies ran while one was open for 6% of the time, Pallas kernels for 0%

commit v1 on v0

--- a/solution.py
+++ b/solution.py
@@ -60,7 +60,7 @@
     assembled = jnp.concatenate([from_below, own_tile, from_above], axis=0)
     owned_squares, peak_total = lax.psum((sum_squares(dosages), peak_squares), "samp")
     variant_total = padded(owned_squares, (("pos", 0),), HALO)
-    cross_total = lax.psum(assembled, "samp")
+    cross_total = jnp.sum(lax.all_gather(assembled, "samp"), axis=0)
     cross_share = lax.dynamic_slice_in_dim(cross_total, own_first, share_rows, 0)
     variant_share = lax.dynamic_slice_in_dim(variant_total, own_first, share_rows, 0)
     variant_index = (

time: 271 us -> 289 us (1.066)
  waiting for transfers between devices: 209 us -> 223 us
  other arithmetic: 10.1 us -> 14.5 us
    all_gather x0 -> x1, waiting for transfers between devices: none -> 60.7 us  [shards(): cross_total = jnp.sum(lax.all_gather(assembled, 'samp'), axis=0)]
    psum x1 -> x0, waiting for transfers between devices: 46.1 us -> none  [shards(): cross_total = lax.psum(assembled, 'samp')]
    reduce_sum x0 -> x1, other arithmetic: none -> 5.6 us  [shards(): cross_total = jnp.sum(lax.all_gather(assembled, 'samp'), axis=0)]
where the time goes in v1:
time: 289 us; the launch traced here: 288 us
  waiting for transfers between devices  223 us (77%)
  starting transfers between devices  18.8 us (7%)
  other arithmetic  14.5 us (5%)
  between operations  13.5 us (5%)
  matrix products  11.5 us (4%)
  blocking collectives  6.96 us (2%)
    ppermute x2, waiting for transfers between devices, padded(): lax.ppermute(tail, axis, [(i, (i + 1) % count) for i in range(ends)])  134 us
    all_gather x1, waiting for transfers between devices, shards(): cross_total = jnp.sum(lax.all_gather(assembled, 'samp'), axis=0)  60.7 us
    ppermute x2, waiting for transfers between devices, from_behind(): return lax.ppermute(array, axis, pairs)  24.7 us
    dot_general x3, matrix products, cross_rows(): lax.dot_general(variant_panel, phenotypes, (((0,), (0,)), ((), ())), pref...  11.5 us
    ppermute x2, starting transfers between devices, padded(): lax.ppermute(tail, axis, [(i, (i + 1) % count) for i in range(ends)])  9.74 us
    psum x1, blocking collectives, shards(): lax.psum((sum_squares(dosages), peak_squares), 'samp')  6.96 us
    ppermute x2, starting transfers between devices, from_behind(): return lax.ppermute(array, axis, pairs)  6.51 us
    reduce_sum x2, other arithmetic, sum_squares(): return jnp.sum(jnp.square(values.astype(jnp.float32)), axis=0)  5.84 us
  transfers between devices with their start and end apart: 7, of which 5 were waited for; matrix products, arithmetic and copies ran while one was open for 6% of the time, Pallas kernels for 0%

profile of v1, /device:TPU:0, one launch (start us, length us, event | category | flops | bytes accessed | tf_op | source)
XLA Modules:
  0.0 288.5 jit_solution(3672579936347686011)
XLA Ops:
  6.5 0.0 all-gather.3.cloned.1.call-start
  6.5 0.0 copy-start
  6.5 5.4 %collective-permute-start.2 = (bf16[4096,384]{1,0:T(8,128)(2,1)}, bf16[4096,384]{1,0:T(8,128)(2,1)S(1)}, u32[]{:S(2)}, u32[]{:S(2)}) collective-permute-start(bf16[4096,384]{1,0:T(8,128)(2,1)} %param.5), channel_id=1, source_target_pairs={{0,1},{1,2},{2,3},{3,4},{4,5},{5,6},{6,7},{8,9},{9,10},{10,11},{11... | collective-permute-start | bytes 9437192 | tf_op jit(solution)/shard_map/ppermute | solution.py:19
  11.9 1.3 collective-permute-start
  13.2 133.6 %collective-permute-done.2 = bf16[4096,384]{1,0:T(8,128)(2,1)S(1)} collective-permute-done((bf16[4096,384]{1,0:T(8,128)(2,1)}, bf16[4096,384]{1,0:T(8,128)(2,1)S(1)}, u32[]{:S(2)}, u32[]{:S(2)}) %collective-permute-start.2) | collective-permute-done | bytes 3145760 | tf_op jit(solution)/shard_map/ppermute | solution.py:19
  146.8 4.5 %fusion = f32[512,384]{1,0:T(8,128)S(1)} fusion(bf16[4096,384]{1,0:T(8,128)(2,1)S(1)} %collective-permute-done.2, bf16[4096,1024]{1,0:T(8,128)(2,1)} %param.4), kind=kOutput, calls=%fused_computation.2 | convolution fusion | flops 1610612736 | bytes 8126464 | tf_op jit(solution)/shard_map/dot_general | solution.py:39
  151.3 0.0 copy-start.1
  151.3 1.6 collective-permute-start.3
  152.9 0.0 collective-permute-done
  152.9 0.0 copy-done
  152.9 2.4 fusion.2
  155.3 5.0 %collective-permute-start.1 = (f32[512,384]{1,0:T(8,128)S(1)}, f32[512,384]{1,0:T(8,128)S(1)}, u32[]{:S(2)}, u32[]{:S(2)}) collective-permute-start(f32[512,384]{1,0:T(8,128)S(1)} %fusion.2), channel_id=1, source_target_pairs={{0,1},{1,2},{2,3},{3,4},{4,5},{5,6},{6,7},{8,9},{9,10},{10,11},{11... | collective-permute-start | bytes 2359304 | tf_op jit(solution)/shard_map/ppermute | solution.py:31
  160.3 0.0 copy-done.1
  160.3 4.5 %fusion.8 = f32[1024,384]{1,0:T(8,128)S(1)} fusion(bf16[4096,1024]{1,0:T(8,128)(2,1)S(1)} %copy-done, bf16[4096,384]{1,0:T(8,128)(2,1)S(1)} %copy-done.1), kind=kOutput, calls=%fused_computation.17 | convolution fusion | flops 3221225472 | bytes 13107200 | tf_op jit(solution)/shard_map/dot_general | solution.py:39
  164.8 7.7 %collective-permute-done.3 = f32[512,384]{1,0:T(8,128)S(1)} collective-permute-done((f32[512,384]{1,0:T(8,128)S(1)}, f32[512,384]{1,0:T(8,128)S(1)}, u32[]{:S(2)}, u32[]{:S(2)}) %collective-permute-start.3) | collective-permute-done | bytes 786464 | tf_op jit(solution)/shard_map/ppermute | solution.py:31
  172.6 17.0 %collective-permute-done.1 = f32[512,384]{1,0:T(8,128)S(1)} collective-permute-done((f32[512,384]{1,0:T(8,128)S(1)}, f32[512,384]{1,0:T(8,128)S(1)}, u32[]{:S(2)}, u32[]{:S(2)}) %collective-permute-start.1) | collective-permute-done | bytes 786464 | tf_op jit(solution)/shard_map/ppermute | solution.py:31
  189.6 1.9 pad_maximum_fusion
  191.4 0.0 all-gather.3.cloned.1.call-update
  191.4 0.8 multiply_reduce_fusion.1
  192.2 5.1 %multiply_reduce_fusion = f32[1024]{0:T(1024)S(1)} fusion(bf16[4096,1024]{1,0:T(8,128)(2,1)} %param.4), kind=kLoop, calls=%fused_computation | loop fusion | flops 12581888 | bytes 8392704 | tf_op jit(solution)/shard_map/reduce_sum | solution.py:35
  197.3 7.0 %all-reduce = (f32[384]{0:T(512)S(1)}, f32[1024]{0:T(1024)S(1)}) all-reduce(f32[384]{0:T(512)S(1)} %multiply_reduce_fusion.1, f32[1024]{0:T(1024)S(1)} %multiply_reduce_fusion), channel_id=1, replica_groups=mesh['samp'=4,'pos'=8] {'samp'}, use_global_device_ids=true, to_apply=%region_4.0 | all-reduce | flops 1408 | bytes 11264 | tf_op jit(solution)/shard_map/psum | solution.py:61
  204.3 4.4 %collective-permute-start.4 = (f32[512]{0:T(512)S(1)}, f32[512]{0:T(512)S(1)}, u32[]{:S(2)}, u32[]{:S(2)}) collective-permute-start(f32[512]{0:T(512)S(1)} %get-tuple-element.8), channel_id=1, source_target_pairs={{0,1},{1,2},{2,3},{3,4},{4,5},{5,6},{6,7},{8,9},{9,10},{10,11},{11... | collective-permute-start | bytes 6152 | tf_op jit(solution)/shard_map/ppermute | solution.py:19
  208.6 1.3 collective-permute-start.5
  210.0 0.0 collective-permute-done.4
  210.0 4.1 %collective-permute-done.5 = f32[512]{0:T(512)S(1)} collective-permute-done((f32[512]{0:T(512)S(1)}, f32[512]{0:T(512)S(1)}, u32[]{:S(2)}, u32[]{:S(2)}) %collective-permute-start.5) | collective-permute-done | bytes 2080 | tf_op jit(solution)/shard_map/ppermute | solution.py:21
  214.1 0.1 fusion.6
  214.2 60.7 %all-gather.3.cloned.1.call-done = f32[8192,384]{1,0:T(8,128)} async-done(((f32[2048,384]{1,0:T(8,128)}), f32[8192,384]{1,0:T(8,128)}) %all-gather.3.cloned.1.call-update) | async-done | bytes 12582928 | tf_op jit(solution)/shard_map/all_gather | solution.py:63
  274.9 0.0 copy-start.2
  274.9 0.0 copy-start.3
  274.9 5.6 %reduce_sum.27 = f32[2048,384]{1,0:T(8,128)S(1)} reduce(f32[4,2048,384]{2,1,0:T(8,128)} %bitcast.7, f32[]{:T(128)} %constant.7.clone.1), dimensions={0}, to_apply=%region_0.0 | reduce | flops 2359296 | bytes 15728644 | tf_op jit(solution)/shard_map/reduce_sum | solution.py:63
  280.5 0.0 copy-done.2
  280.5 0.0 copy-done.3
  280.5 1.2 select_bitcast_fusion
  (3 shorter events, 0.0 us)
Async XLA Ops:
  6.5 268.3 %all-gather.3.cloned.1.call-start = ((), (), s32[]{:S(2)}) async-start(), calls=%async_computation | async-start | bytes 15728640 | tf_op jit(solution)/shard_map/all_gather | solution.py:63
  6.5 146.4 %copy-start = (bf16[4096,1024]{1,0:T(8,128)(2,1)S(1)}, bf16[4096,1024]{1,0:T(8,128)(2,1)}, u32[]{:S(2)}) copy-start(bf16[4096,1024]{1,0:T(8,128)(2,1)} %param.4) | copy-start | bytes 25165828
  6.5 140.2 %collective-permute-start.2 = (bf16[4096,384]{1,0:T(8,128)(2,1)}, bf16[4096,384]{1,0:T(8,128)(2,1)S(1)}, u32[]{:S(2)}, u32[]{:S(2)}) collective-permute-start(bf16[4096,384]{1,0:T(8,128)(2,1)} %param.5), channel_id=1, source_target_pairs={{0,1},{1,2},{2,3},{3,4},{4,5},{5,6},{6,7},{8,9},{9,10},{10,11},{11... | collective-permute-start | bytes 9437192 | tf_op jit(solution)/shard_map/ppermute | solution.py:19
  11.9 141.0 %collective-permute-start = (bf16[4096,384]{1,0:T(8,128)(2,1)}, bf16[4096,384]{1,0:T(8,128)(2,1)S(1)}, u32[]{:S(2)}, u32[]{:S(2)}) collective-permute-start(bf16[4096,384]{1,0:T(8,128)(2,1)} %param.5), channel_id=1, source_target_pairs={{1,0},{2,1},{3,2},{4,3},{5,4},{6,5},{7,6},{9,8},{10,9},{11,10},{12... | collective-permute-start | bytes 9437192 | tf_op jit(solution)/shard_map/ppermute | solution.py:21
  151.3 9.0 %copy-start.1 = (bf16[4096,384]{1,0:T(8,128)(2,1)S(1)}, bf16[4096,384]{1,0:T(8,128)(2,1)}, u32[]{:S(2)}) copy-start(bf16[4096,384]{1,0:T(8,128)(2,1)} %param.5) | copy-start | bytes 9437188
  151.3 21.2 %collective-permute-start.3 = (f32[512,384]{1,0:T(8,128)S(1)}, f32[512,384]{1,0:T(8,128)S(1)}, u32[]{:S(2)}, u32[]{:S(2)}) collective-permute-start(f32[512,384]{1,0:T(8,128)S(1)} %fusion), channel_id=1, source_target_pairs={{1,0},{2,1},{3,2},{4,3},{5,4},{6,5},{7,6},{9,8},{10,9},{11,10},{12... | collective-permute-start | bytes 2359304 | tf_op jit(solution)/shard_map/ppermute | solution.py:31
  155.3 34.2 %collective-permute-start.1 = (f32[512,384]{1,0:T(8,128)S(1)}, f32[512,384]{1,0:T(8,128)S(1)}, u32[]{:S(2)}, u32[]{:S(2)}) collective-permute-start(f32[512,384]{1,0:T(8,128)S(1)} %fusion.2), channel_id=1, source_target_pairs={{0,1},{1,2},{2,3},{3,4},{4,5},{5,6},{6,7},{8,9},{9,10},{10,11},{11... | collective-permute-start | bytes 2359304 | tf_op jit(solution)/shard_map/ppermute | solution.py:31
  204.3 5.7 %collective-permute-start.4 = (f32[512]{0:T(512)S(1)}, f32[512]{0:T(512)S(1)}, u32[]{:S(2)}, u32[]{:S(2)}) collective-permute-start(f32[512]{0:T(512)S(1)} %get-tuple-element.8), channel_id=1, source_target_pairs={{0,1},{1,2},{2,3},{3,4},{4,5},{5,6},{6,7},{8,9},{9,10},{10,11},{11... | collective-permute-start | bytes 6152 | tf_op jit(solution)/shard_map/ppermute | solution.py:19
  208.6 5.5 %collective-permute-start.5 = (f32[512]{0:T(512)S(1)}, f32[512]{0:T(512)S(1)}, u32[]{:S(2)}, u32[]{:S(2)}) collective-permute-start(f32[512]{0:T(512)S(1)} %get-tuple-element.7), channel_id=1, source_target_pairs={{1,0},{2,1},{3,2},{4,3},{5,4},{6,5},{7,6},{9,8},{10,9},{11,10},{12... | collective-permute-start | bytes 6152 | tf_op jit(solution)/shard_map/ppermute | solution.py:21
  274.9 5.6 %copy-start.2 = (s32[384]{0:T(512)S(1)}, s32[384]{0:T(512)}, u32[]{:S(2)}) copy-start(s32[384]{0:T(512)} %param.7) | copy-start | bytes 4612
  274.9 5.6 %copy-start.3 = (s32[384]{0:T(512)S(1)}, s32[384]{0:T(512)}, u32[]{:S(2)}) copy-start(s32[384]{0:T(512)} %param.6) | copy-start | bytes 4612
Sparse Core Ops, SparseCore 0:
  191.6 83.2 all-gather.2
